TPU v7x, 512 devices: a whole 4x4x16 slice. The times are simulated.
512 devices in a mesh: ctx: 64 (over y, z), head: 8 (over x, core).
Axes of the slice: x: 4, y: 4, z: 16, core: 2. Of those that a mesh axis runs over, the one named last changes fastest.
Arguments:
- queries: bfloat16 [32768, 4096], P(('ctx', 'head')), may hold values from -12 to 12
- keys: bfloat16 [32768, 1024], P(('ctx', 'head')), may hold values from -12 to 12
- values: bfloat16 [32768, 1024], P(('ctx', 'head')), may hold values from -6 to 6
- doc_lengths: int32 [16], replicated, may hold values from 1 to 4096, 32768 in all
- piece_owner: int32 [64, 64], P('ctx'), may hold values from 0 to 63, each once within a row
Outputs:
- owned: bfloat16 [32768, 4096], P('ctx', 'head')
Inputs may be any that keep to these rules, and one draw needn't show every extreme that they name: Each row of piece_owner is a permutation of 0 .. 63. doc_lengths sum to 32768, and the largest equals 4096.
All inputs are finite; a program needn't handle non-finite values.
Results may differ from a plain program's by a relative error of at most 0.0033.
Values may be sent and summed in bfloat16 or wider, within the bound.
A program may use at most 64 MiB of HBM per device.

v0:
```python
import math
import jax
import jax.numpy as jnp
from jax import lax
from jax.sharding import PartitionSpec as P

HD = 128
QPK = 4
MOST = 4096
masked_score = -1e30


def passed_along(value, axis, steps):
    count = lax.axis_size(axis)
    leading, last = (max(0, -steps), min(count, count - steps))
    return lax.ppermute(value, axis, [(source, source + steps) for source in range(leading, last)])


def doc_index(positions, doc_lengths):
    doc_ends = jnp.cumsum(doc_lengths)
    return jnp.sum((positions[:, None] >= doc_ends[None, :]).astype(jnp.int32), axis=1)


def per_device(queries, keys, values, doc_lengths, piece_owner):
    query_rows, key_rows, value_rows = (
        lax.all_to_all(queries, "head", split_axis=1, concat_axis=0, tiled=True),
        lax.all_to_all(keys, "head", split_axis=1, concat_axis=0, tiled=True),
        lax.all_to_all(values, "head", split_axis=1, concat_axis=0, tiled=True),
    )
    tokens_here = query_rows.shape[0]
    groups = key_rows.shape[1] // HD
    features = query_rows.shape[1]
    reach_back = (MOST - 1) // tokens_here + 1
    score_scale = 1.0 / math.sqrt(HD)
    ctx_place = lax.axis_index("ctx")
    offsets = jnp.arange(tokens_here, dtype=jnp.int32)
    query_position = ctx_place * tokens_here + offsets
    query_ids = doc_index(query_position, doc_lengths)
    paired = jnp.stack([key_rows, value_rows])
    shards = [paired]
    for distance in range(1, reach_back + 1):
        shards.append(passed_along(paired, "ctx", distance))
    key_positions = []
    key_ids = []
    for distance in range(reach_back + 1):
        shard_position = (ctx_place - distance) * tokens_here + offsets
        key_positions.append(shard_position)
        key_ids.append(doc_index(shard_position, doc_lengths))
    block_rows = 512
    block_count = tokens_here // block_rows
    query_split = query_rows.reshape(block_count, block_rows, groups, QPK, HD)
    position_split = query_position.reshape(block_count, block_rows)
    ids_split = query_ids.reshape(block_count, block_rows)

    def attend(operands):
        query_block, position_block, ids_block = operands
        row_top = jnp.full((block_rows, groups, QPK), masked_score, jnp.float32)
        row_total = jnp.zeros((block_rows, groups, QPK), jnp.float32)
        weighted = jnp.zeros((block_rows, groups, QPK, HD), jnp.float32)
        carry_state = (row_top, row_total, weighted)
        for distance in range(reach_back + 1):
            shard_pair = shards[distance]
            shard_keys = shard_pair[0].reshape(tokens_here, groups, HD)
            shard_values = shard_pair[1].reshape(tokens_here, groups, HD)
            live_pairs = (
                (key_positions[distance][None, :] >= 0)
                & (key_positions[distance][None, :] <= position_block[:, None])
                & (key_ids[distance][None, :] == ids_block[:, None])
            )

            def update(
                state_now, shard_keys=shard_keys, shard_values=shard_values, live_pairs=live_pairs
            ):
                old_top, old_total, old_weighted = state_now
                live_mask = live_pairs[:, None, None, :]
                scores = (
                    jnp.einsum(
                        "qgjd,kgd->qgjk",
                        query_block,
                        shard_keys,
                        preferred_element_type=jnp.float32,
                    )
                    * score_scale
                )
                scores = jnp.where(live_mask, scores, masked_score)
                new_top = jnp.maximum(old_top, jnp.max(scores, axis=-1))
                factor = jnp.exp(old_top - new_top)
                weights = jnp.where(live_mask, jnp.exp(scores - new_top[..., None]), 0.0)
                new_total = old_total * factor + jnp.sum(weights, axis=-1)
                new_weighted = old_weighted * factor[..., None] + jnp.einsum(
                    "qgjk,kgd->qgjd",
                    weights.astype(jnp.bfloat16),
                    shard_values,
                    preferred_element_type=jnp.float32,
                )
                return (new_top, new_total, new_weighted)

            carry_state = update(carry_state)
        final_top, final_total, final_weighted = carry_state
        result = final_weighted / final_total[..., None]
        return result.astype(jnp.bfloat16).reshape(block_rows, groups * QPK * HD)

    attended = lax.map(attend, (query_split, position_split, ids_split)).reshape(
        tokens_here, features
    )
    ctx_count = lax.axis_size("ctx")
    piece_rows = tokens_here // ctx_count
    owner_row = piece_owner[0]
    slot_index = jnp.arange(ctx_count, dtype=jnp.int32)
    matches = owner_row[:, None] == slot_index[None, :]
    inverse = jnp.sum(jnp.where(matches, slot_index[:, None], 0), axis=0)
    pieces = attended.reshape(ctx_count, piece_rows, features)
    ordered = jnp.take(pieces, inverse, axis=0)
    received = lax.all_to_all(ordered, "ctx", split_axis=0, concat_axis=0, tiled=True)
    return received.reshape(tokens_here, features)


def solution(mesh):
    return jax.shard_map(
        per_device,
        mesh=mesh,
        in_specs=(
            P(("ctx", "head"), None),
            P(("ctx", "head"), None),
            P(("ctx", "head"), None),
            P(),
            P("ctx", None),
        ),
        out_specs=P("ctx", "head"),
        check_vma=False,
    )
```

profile of v0, /device:TPU:4, one launch (start us, length us, event | category | flops | bytes accessed | tf_op | source)
XLA Modules:
  0.0 324.6 jit_solution(12941780340591550754)
XLA Ops:
  1.6 9.1 %all-to-all-start = ((bf16[64,8,128]{2,0,1:T(8,128)(2,1)}), bf16[64,8,128]{2,0,1:T(8,128)(2,1)S(1)}, u32[]{:S(2)}, u32[]{:S(2)}) async-start(bf16[64,8,128]{2,0,1:T(8,128)(2,1)} %copy_bitcast_fusion.2), calls=%async_computation | async-start | bytes 262144 | tf_op jit(solution)/shard_map/all_to_all | solution.py:27
  12.5 1.6 copy_bitcast_fusion.1
  14.2 2.7 compare_and_fusion.8
  17.0 4.8 %all-to-all-start.2 = ((bf16[64,8,128]{2,0,1:T(8,128)(2,1)}), bf16[64,8,128]{2,0,1:T(8,128)(2,1)S(1)}, u32[]{:S(2)}, u32[]{:S(2)}) async-start(bf16[64,8,128]{2,0,1:T(8,128)(2,1)} %copy_bitcast_fusion.1), calls=%async_computation.2 | async-start | bytes 262144 | tf_op jit(solution)/shard_map/all_to_all | solution.py:28
  21.8 1.9 copy.187
  23.7 1.5 all-to-all-done.2
  25.2 6.1 %all-to-all-start.1 = ((bf16[64,8,512]{2,0,1:T(8,128)(2,1)}), bf16[64,8,512]{2,0,1:T(8,128)(2,1)S(1)}, u32[]{:S(2)}, u32[]{:S(2)}) async-start(bf16[64,8,512]{2,0,1:T(8,128)(2,1)} %bitcast.463), calls=%async_computation.1 | async-start | bytes 1048576 | tf_op jit(solution)/shard_map/all_to_all | solution.py:26
  33.3 12.1 %collective-permute-start.7 = (bf16[2,512,128]{2,1,0:T(8,128)(2,1)}, bf16[2,512,128]{2,1,0:T(8,128)(2,1)}, u32[]{:S(2)}, u32[]{:S(2)}) collective-permute-start(bf16[2,512,128]{2,1,0:T(8,128)(2,1)} %pad_maximum_fusion), channel_id=1, source_target_pairs={{0,64},{8,72},{16,80},{24,88},{32,96},{40,104},{48,112},{56,120},{... | collective-permute-start | bytes 786440 | tf_op jit(solution)/shard_map/ppermute | solution.py:16
  45.3 6.4 %collective-permute-start.6 = (bf16[2,512,128]{2,1,0:T(8,128)(2,1)}, bf16[2,512,128]{2,1,0:T(8,128)(2,1)}, u32[]{:S(2)}, u32[]{:S(2)}) collective-permute-start(bf16[2,512,128]{2,1,0:T(8,128)(2,1)} %pad_maximum_fusion), channel_id=1, source_target_pairs={{0,56},{8,64},{16,72},{24,80},{32,88},{40,96},{48,104},{56,112},{6... | collective-permute-start | bytes 786440 | tf_op jit(solution)/shard_map/ppermute | solution.py:16
  51.7 4.7 %collective-permute-start.5 = (bf16[2,512,128]{2,1,0:T(8,128)(2,1)}, bf16[2,512,128]{2,1,0:T(8,128)(2,1)}, u32[]{:S(2)}, u32[]{:S(2)}) collective-permute-start(bf16[2,512,128]{2,1,0:T(8,128)(2,1)} %pad_maximum_fusion), channel_id=1, source_target_pairs={{0,48},{8,56},{16,64},{24,72},{32,80},{40,88},{48,96},{56,104},{64... | collective-permute-start | bytes 786440 | tf_op jit(solution)/shard_map/ppermute | solution.py:16
  56.4 8.6 %collective-permute-start.4 = (bf16[2,512,128]{2,1,0:T(8,128)(2,1)}, bf16[2,512,128]{2,1,0:T(8,128)(2,1)}, u32[]{:S(2)}, u32[]{:S(2)}) collective-permute-start(bf16[2,512,128]{2,1,0:T(8,128)(2,1)} %pad_maximum_fusion), channel_id=1, source_target_pairs={{0,40},{8,48},{16,56},{24,64},{32,72},{40,80},{48,88},{56,96},{64,... | collective-permute-start | bytes 786440 | tf_op jit(solution)/shard_map/ppermute | solution.py:16
  65.0 3.4 %collective-permute-start.1 = (bf16[2,512,128]{2,1,0:T(8,128)(2,1)}, bf16[2,512,128]{2,1,0:T(8,128)(2,1)}, u32[]{:S(2)}, u32[]{:S(2)}) collective-permute-start(bf16[2,512,128]{2,1,0:T(8,128)(2,1)} %pad_maximum_fusion), channel_id=1, source_target_pairs={{0,16},{8,24},{16,32},{24,40},{32,48},{40,56},{48,64},{56,72},{64,... | collective-permute-start | bytes 786440 | tf_op jit(solution)/shard_map/ppermute | solution.py:16
  69.4 109.8 %collective-permute-done.1 = bf16[2,512,128]{2,1,0:T(8,128)(2,1)} collective-permute-done((bf16[2,512,128]{2,1,0:T(8,128)(2,1)}, bf16[2,512,128]{2,1,0:T(8,128)(2,1)}, u32[]{:S(2)}, u32[]{:S(2)}) %collective-permute-start.1) | collective-permute-done | bytes 262176 | tf_op jit(solution)/shard_map/ppermute | solution.py:16
  179.2 5.8 %collective-permute-start.2 = (bf16[2,512,128]{2,1,0:T(8,128)(2,1)}, bf16[2,512,128]{2,1,0:T(8,128)(2,1)S(1)}, u32[]{:S(2)}, u32[]{:S(2)}) collective-permute-start(bf16[2,512,128]{2,1,0:T(8,128)(2,1)} %pad_maximum_fusion), channel_id=1, source_target_pairs={{0,24},{8,32},{16,40},{24,48},{32,56},{40,64},{48,72},{56,80},{64,... | collective-permute-start | bytes 786440 | tf_op jit(solution)/shard_map/ppermute | solution.py:16
  185.0 1.8 fusion.2
  186.8 10.9 %collective-permute-done.2 = bf16[2,512,128]{2,1,0:T(8,128)(2,1)S(1)} collective-permute-done((bf16[2,512,128]{2,1,0:T(8,128)(2,1)}, bf16[2,512,128]{2,1,0:T(8,128)(2,1)S(1)}, u32[]{:S(2)}, u32[]{:S(2)}) %collective-permute-start.2) | collective-permute-done | bytes 262176 | tf_op jit(solution)/shard_map/ppermute | solution.py:16
  197.7 11.1 %collective-permute-start.3 = (bf16[2,512,128]{2,1,0:T(8,128)(2,1)}, bf16[2,512,128]{2,1,0:T(8,128)(2,1)S(1)}, u32[]{:S(2)}, u32[]{:S(2)}) collective-permute-start(bf16[2,512,128]{2,1,0:T(8,128)(2,1)} %pad_maximum_fusion), channel_id=1, source_target_pairs={{0,32},{8,40},{16,48},{24,56},{32,64},{40,72},{48,80},{56,88},{64,... | collective-permute-start | bytes 786440 | tf_op jit(solution)/shard_map/ppermute | solution.py:16
  209.7 7.8 %collective-permute-done.3 = bf16[2,512,128]{2,1,0:T(8,128)(2,1)S(1)} collective-permute-done((bf16[2,512,128]{2,1,0:T(8,128)(2,1)}, bf16[2,512,128]{2,1,0:T(8,128)(2,1)S(1)}, u32[]{:S(2)}, u32[]{:S(2)}) %collective-permute-start.3) | collective-permute-done | bytes 262176 | tf_op jit(solution)/shard_map/ppermute | solution.py:16
  217.5 9.1 %collective-permute-start = (bf16[2,512,128]{2,1,0:T(8,128)(2,1)}, bf16[2,512,128]{2,1,0:T(8,128)(2,1)S(1)}, u32[]{:S(2)}, u32[]{:S(2)}) collective-permute-start(bf16[2,512,128]{2,1,0:T(8,128)(2,1)} %pad_maximum_fusion), channel_id=1, source_target_pairs={{0,8},{8,16},{16,24},{24,32},{32,40},{40,48},{48,56},{56,64},{64,7... | collective-permute-start | bytes 786440 | tf_op jit(solution)/shard_map/ppermute | solution.py:16
  227.5 1.8 fusion.5
  229.3 1.8 fusion.6
  231.1 5.2 %collective-permute-done = bf16[2,512,128]{2,1,0:T(8,128)(2,1)S(1)} collective-permute-done((bf16[2,512,128]{2,1,0:T(8,128)(2,1)}, bf16[2,512,128]{2,1,0:T(8,128)(2,1)S(1)}, u32[]{:S(2)}, u32[]{:S(2)}) %collective-permute-start) | collective-permute-done | bytes 262176 | tf_op jit(solution)/shard_map/ppermute | solution.py:16
  237.2 1.8 fusion.7
  239.0 1.8 fusion.8
  250.6 2.1 fusion.93
  252.7 2.4 fusion.66
  255.1 2.4 fusion.69
  257.5 2.4 fusion.72
  262.9 2.4 fusion.81
  265.4 3.1 fusion.141
  268.5 2.9 divide_convert_fusion
  272.8 50.9 %all_to_all.53 = bf16[64,8,512]{2,1,0:T(8,128)(2,1)S(1)} all-to-all(bf16[64,8,512]{2,1,0:T(8,128)(2,1)S(1)} %broadcast_select_fusion), channel_id=1, replica_groups=mesh['ctx'=64,'head'=8] {'ctx'}, dimensions={0} | all-to-all | bytes 1048576 | tf_op jit(solution)/shard_map/all_to_all | solution.py:114
  (66 shorter events, 24.0 us)
Async XLA Ops:
  0.0 0.9 copy-start
  1.6 15.4 %all-to-all-start = ((bf16[64,8,128]{2,0,1:T(8,128)(2,1)}), bf16[64,8,128]{2,0,1:T(8,128)(2,1)S(1)}, u32[]{:S(2)}, u32[]{:S(2)}) async-start(bf16[64,8,128]{2,0,1:T(8,128)(2,1)} %copy_bitcast_fusion.2), calls=%async_computation | async-start | bytes 262144 | tf_op jit(solution)/shard_map/all_to_all | solution.py:27
  17.0 8.2 %all-to-all-start.2 = ((bf16[64,8,128]{2,0,1:T(8,128)(2,1)}), bf16[64,8,128]{2,0,1:T(8,128)(2,1)S(1)}, u32[]{:S(2)}, u32[]{:S(2)}) async-start(bf16[64,8,128]{2,0,1:T(8,128)(2,1)} %copy_bitcast_fusion.1), calls=%async_computation.2 | async-start | bytes 262144 | tf_op jit(solution)/shard_map/all_to_all | solution.py:28
  25.2 43.2 %all-to-all-start.1 = ((bf16[64,8,512]{2,0,1:T(8,128)(2,1)}), bf16[64,8,512]{2,0,1:T(8,128)(2,1)S(1)}, u32[]{:S(2)}, u32[]{:S(2)}) async-start(bf16[64,8,512]{2,0,1:T(8,128)(2,1)} %bitcast.463), calls=%async_computation.1 | async-start | bytes 1048576 | tf_op jit(solution)/shard_map/all_to_all | solution.py:26
  33.3 205.8 %collective-permute-start.7 = (bf16[2,512,128]{2,1,0:T(8,128)(2,1)}, bf16[2,512,128]{2,1,0:T(8,128)(2,1)}, u32[]{:S(2)}, u32[]{:S(2)}) collective-permute-start(bf16[2,512,128]{2,1,0:T(8,128)(2,1)} %pad_maximum_fusion), channel_id=1, source_target_pairs={{0,64},{8,72},{16,80},{24,88},{32,96},{40,104},{48,112},{56,120},{... | collective-permute-start | bytes 786440 | tf_op jit(solution)/shard_map/ppermute | solution.py:16
  45.3 191.9 %collective-permute-start.6 = (bf16[2,512,128]{2,1,0:T(8,128)(2,1)}, bf16[2,512,128]{2,1,0:T(8,128)(2,1)}, u32[]{:S(2)}, u32[]{:S(2)}) collective-permute-start(bf16[2,512,128]{2,1,0:T(8,128)(2,1)} %pad_maximum_fusion), channel_id=1, source_target_pairs={{0,56},{8,64},{16,72},{24,80},{32,88},{40,96},{48,104},{56,112},{6... | collective-permute-start | bytes 786440 | tf_op jit(solution)/shard_map/ppermute | solution.py:16
  51.7 177.6 %collective-permute-start.5 = (bf16[2,512,128]{2,1,0:T(8,128)(2,1)}, bf16[2,512,128]{2,1,0:T(8,128)(2,1)}, u32[]{:S(2)}, u32[]{:S(2)}) collective-permute-start(bf16[2,512,128]{2,1,0:T(8,128)(2,1)} %pad_maximum_fusion), channel_id=1, source_target_pairs={{0,48},{8,56},{16,64},{24,72},{32,80},{40,88},{48,96},{56,104},{64... | collective-permute-start | bytes 786440 | tf_op jit(solution)/shard_map/ppermute | solution.py:16
  56.4 171.1 %collective-permute-start.4 = (bf16[2,512,128]{2,1,0:T(8,128)(2,1)}, bf16[2,512,128]{2,1,0:T(8,128)(2,1)}, u32[]{:S(2)}, u32[]{:S(2)}) collective-permute-start(bf16[2,512,128]{2,1,0:T(8,128)(2,1)} %pad_maximum_fusion), channel_id=1, source_target_pairs={{0,40},{8,48},{16,56},{24,64},{32,72},{40,80},{48,88},{56,96},{64,... | collective-permute-start | bytes 786440 | tf_op jit(solution)/shard_map/ppermute | solution.py:16
  65.0 114.2 %collective-permute-start.1 = (bf16[2,512,128]{2,1,0:T(8,128)(2,1)}, bf16[2,512,128]{2,1,0:T(8,128)(2,1)}, u32[]{:S(2)}, u32[]{:S(2)}) collective-permute-start(bf16[2,512,128]{2,1,0:T(8,128)(2,1)} %pad_maximum_fusion), channel_id=1, source_target_pairs={{0,16},{8,24},{16,32},{24,40},{32,48},{40,56},{48,64},{56,72},{64,... | collective-permute-start | bytes 786440 | tf_op jit(solution)/shard_map/ppermute | solution.py:16
  179.2 18.5 %collective-permute-start.2 = (bf16[2,512,128]{2,1,0:T(8,128)(2,1)}, bf16[2,512,128]{2,1,0:T(8,128)(2,1)S(1)}, u32[]{:S(2)}, u32[]{:S(2)}) collective-permute-start(bf16[2,512,128]{2,1,0:T(8,128)(2,1)} %pad_maximum_fusion), channel_id=1, source_target_pairs={{0,24},{8,32},{16,40},{24,48},{32,56},{40,64},{48,72},{56,80},{64,... | collective-permute-start | bytes 786440 | tf_op jit(solution)/shard_map/ppermute | solution.py:16
  197.7 29.8 %copy-start.4 = (bf16[2,512,128]{2,1,0:T(8,128)(2,1)}, bf16[2,512,128]{2,1,0:T(8,128)(2,1)S(1)}, u32[]{:S(2)}) copy-start(bf16[2,512,128]{2,1,0:T(8,128)(2,1)S(1)} %collective-permute-done.2) | copy-start | bytes 786436
  197.7 19.8 %collective-permute-start.3 = (bf16[2,512,128]{2,1,0:T(8,128)(2,1)}, bf16[2,512,128]{2,1,0:T(8,128)(2,1)S(1)}, u32[]{:S(2)}, u32[]{:S(2)}) collective-permute-start(bf16[2,512,128]{2,1,0:T(8,128)(2,1)} %pad_maximum_fusion), channel_id=1, source_target_pairs={{0,32},{8,40},{16,48},{24,56},{32,64},{40,72},{48,80},{56,88},{64,... | collective-permute-start | bytes 786440 | tf_op jit(solution)/shard_map/ppermute | solution.py:16
  217.5 11.8 %copy-start.6 = (bf16[2,512,128]{2,1,0:T(8,128)(2,1)}, bf16[2,512,128]{2,1,0:T(8,128)(2,1)S(1)}, u32[]{:S(2)}) copy-start(bf16[2,512,128]{2,1,0:T(8,128)(2,1)S(1)} %collective-permute-done.3) | copy-start | bytes 786436
  217.5 18.8 %collective-permute-start = (bf16[2,512,128]{2,1,0:T(8,128)(2,1)}, bf16[2,512,128]{2,1,0:T(8,128)(2,1)S(1)}, u32[]{:S(2)}, u32[]{:S(2)}) collective-permute-start(bf16[2,512,128]{2,1,0:T(8,128)(2,1)} %pad_maximum_fusion), channel_id=1, source_target_pairs={{0,8},{8,16},{16,24},{24,32},{32,40},{40,48},{48,56},{56,64},{64,7... | collective-permute-start | bytes 786440 | tf_op jit(solution)/shard_map/ppermute | solution.py:16
  226.6 2.8 copy-start.1
  236.3 2.7 copy-start.2
  257.5 2.4 copy-start.7
  259.9 1.5 copy-start.5
  262.9 2.4 copy-start.3
where the time goes:
time: 325 us
  waiting for transfers between devices  135 us (42%)
  starting transfers between devices  81.1 us (25%)
  blocking collectives  50.9 us (16%)
  matrix products  33.3 us (10%)
  other arithmetic  15.7 us (5%)
  local copies, waits for them, and re-layouts  7.92 us (2%)
    ppermute x8, waiting for transfers between devices, passed_along(): lax.ppermute(value, axis, [(source, source + steps) for source in range(l...  134 us
    ppermute x8, starting transfers between devices, passed_along(): lax.ppermute(value, axis, [(source, source + steps) for source in range(l...  61.1 us
    all_to_all x1, blocking collectives, per_device(): lax.all_to_all(ordered, 'ctx', split_axis=0, concat_axis=0, tiled=True)  50.9 us
    dot_general x9, matrix products, update(): jnp.einsum('qgjk,kgd->qgjd', weights.astype(jnp.bfloat16), shard_values,...  20.7 us
    dot_general x9, matrix products, update(): jnp.einsum('qgjd,kgd->qgjk', query_block, shard_keys, preferred_element_t...  12.6 us
    reduce_sum x9, other arithmetic, update(): new_total = old_total * factor + jnp.sum(weights, axis=-1)  9.67 us
    all_to_all x1, starting transfers between devices, per_device(): lax.all_to_all(keys, 'head', split_axis=1, concat_axis=0, tiled=True)  9.15 us
  transfers between devices with their start and end apart: 11, of which 5 were waited for; matrix products, arithmetic and copies ran while one was open for 6% of the time, Pallas kernels for 0%

commit v1 on v0

--- a/solution.py
+++ b/solution.py
@@ -8,6 +8,16 @@
 QPK = 4
 MOST = 4096
 masked_score = -1e30
+
+
+def time_weights(mine_x):
+    mixed_arr = jnp.concatenate(
+        jax.lax.all_to_all(
+            jnp.stack(jnp.split(mine_x, jax.lax.axis_size("head"), axis=1)), "head", 0, 0
+        ),
+        axis=0,
+    )
+    return mixed_arr
 
 
 def passed_along(value, axis, steps):
@@ -24,7 +34,7 @@
 def per_device(queries, keys, values, doc_lengths, piece_owner):
     query_rows, key_rows, value_rows = (
         lax.all_to_all(queries, "head", split_axis=1, concat_axis=0, tiled=True),
-        lax.all_to_all(keys, "head", split_axis=1, concat_axis=0, tiled=True),
+        time_weights(keys),
         lax.all_to_all(values, "head", split_axis=1, concat_axis=0, tiled=True),
     )
     tokens_here = query_rows.shape[0]

time: 325 us -> 335 us (1.031)
  local copies, waits for them, and re-layouts: 7.92 us -> 16.9 us
    unnamed x17 -> x24, local copies, waits for them, and re-layouts: 1.73 us -> 10.9 us
    all_to_all x1, starting transfers between devices: 9.15 us -> 4.8 us  [time_weights(): jax.lax.all_to_all(jnp.stack(jnp.split(mine_x, jax.lax.axis_size('head'),...]
    all_to_all x1, starting transfers between devices: 4.8 us -> 9.15 us  [per_device(): lax.all_to_all(values, 'head', split_axis=1, concat_axis=0, tiled=True)]
  transfers between devices with their start and end apart: 11 -> 11, of which waited for: 5 -> 5; matrix products, arithmetic and copies ran while one was open for 6% -> 9% of each run, Pallas kernels for 0% -> 0%
where the time goes in v1:
time: 335 us; the launch traced here: 334 us
  waiting for transfers between devices  135 us (40%)
  starting transfers between devices  81.1 us (24%)
  blocking collectives  50.9 us (15%)
  matrix products  33.4 us (10%)
  local copies, waits for them, and re-layouts  16.9 us (5%)
  other arithmetic  15.7 us (5%)
    ppermute x8, waiting for transfers between devices, passed_along(): lax.ppermute(value, axis, [(source, source + steps) for source in range(l...  134 us
    ppermute x8, starting transfers between devices, passed_along(): lax.ppermute(value, axis, [(source, source + steps) for source in range(l...  61.1 us
    all_to_all x1, blocking collectives, per_device(): lax.all_to_all(ordered, 'ctx', split_axis=0, concat_axis=0, tiled=True)  50.9 us
    dot_general x9, matrix products, update(): jnp.einsum('qgjk,kgd->qgjd', weights.astype(jnp.bfloat16), shard_values,...  20.8 us
    dot_general x9, matrix products, update(): jnp.einsum('qgjd,kgd->qgjk', query_block, shard_keys, preferred_element_t...  12.6 us
    unnamed x24, local copies, waits for them, and re-layouts  10.9 us
    reduce_sum x9, other arithmetic, update(): new_total = old_total * factor + jnp.sum(weights, axis=-1)  9.65 us
    all_to_all x1, starting transfers between devices, per_device(): lax.all_to_all(values, 'head', split_axis=1, concat_axis=0, tiled=True)  9.15 us
  transfers between devices with their start and end apart: 11, of which 5 were waited for; matrix products, arithmetic and copies ran while one was open for 9% of the time, Pallas kernels for 0%

profile of v1, /device:TPU:4, one launch (start us, length us, event | category | flops | bytes accessed | tf_op | source)
XLA Modules:
  0.0 333.6 jit_solution(10061666812885193452)
XLA Ops:
  1.6 9.1 %all-to-all-start.2 = ((bf16[64,8,128]{2,0,1:T(8,128)(2,1)}), bf16[64,8,128]{2,0,1:T(8,128)(2,1)S(1)}, u32[]{:S(2)}, u32[]{:S(2)}) async-start(bf16[64,8,128]{2,0,1:T(8,128)(2,1)} %copy_bitcast_fusion.1), calls=%async_computation.2 | async-start | bytes 262144 | tf_op jit(solution)/shard_map/all_to_all | solution.py:38
  23.2 2.7 compare_and_fusion.8
  25.9 4.8 %all-to-all-start = ((bf16[8,64,128]{2,1,0:T(8,128)(2,1)}), bf16[8,64,128]{2,1,0:T(8,128)(2,1)S(1)}, u32[]{:S(2)}, u32[]{:S(2)}) async-start(bf16[8,64,128]{2,1,0:T(8,128)(2,1)} %constant_dynamic-update-slice_fusion), calls=%async_computation | async-start | bytes 262144 | tf_op jit(solution)/shard_map/all_to_all | solution.py:15
  30.7 1.9 copy.182
  32.6 1.5 all-to-all-done
  34.1 6.1 %all-to-all-start.1 = ((bf16[64,8,512]{2,0,1:T(8,128)(2,1)}), bf16[64,8,512]{2,0,1:T(8,128)(2,1)S(1)}, u32[]{:S(2)}, u32[]{:S(2)}) async-start(bf16[64,8,512]{2,0,1:T(8,128)(2,1)} %bitcast.471), calls=%async_computation.1 | async-start | bytes 1048576 | tf_op jit(solution)/shard_map/all_to_all | solution.py:36
  42.2 12.1 %collective-permute-start.7 = (bf16[2,512,128]{2,1,0:T(8,128)(2,1)}, bf16[2,512,128]{2,1,0:T(8,128)(2,1)}, u32[]{:S(2)}, u32[]{:S(2)}) collective-permute-start(bf16[2,512,128]{2,1,0:T(8,128)(2,1)} %pad_maximum_fusion), channel_id=1, source_target_pairs={{0,64},{8,72},{16,80},{24,88},{32,96},{40,104},{48,112},{56,120},{... | collective-permute-start | bytes 786440 | tf_op jit(solution)/shard_map/ppermute | solution.py:26
  54.3 6.4 %collective-permute-start.6 = (bf16[2,512,128]{2,1,0:T(8,128)(2,1)}, bf16[2,512,128]{2,1,0:T(8,128)(2,1)}, u32[]{:S(2)}, u32[]{:S(2)}) collective-permute-start(bf16[2,512,128]{2,1,0:T(8,128)(2,1)} %pad_maximum_fusion), channel_id=1, source_target_pairs={{0,56},{8,64},{16,72},{24,80},{32,88},{40,96},{48,104},{56,112},{6... | collective-permute-start | bytes 786440 | tf_op jit(solution)/shard_map/ppermute | solution.py:26
  60.7 4.7 %collective-permute-start.5 = (bf16[2,512,128]{2,1,0:T(8,128)(2,1)}, bf16[2,512,128]{2,1,0:T(8,128)(2,1)}, u32[]{:S(2)}, u32[]{:S(2)}) collective-permute-start(bf16[2,512,128]{2,1,0:T(8,128)(2,1)} %pad_maximum_fusion), channel_id=1, source_target_pairs={{0,48},{8,56},{16,64},{24,72},{32,80},{40,88},{48,96},{56,104},{64... | collective-permute-start | bytes 786440 | tf_op jit(solution)/shard_map/ppermute | solution.py:26
  65.3 8.6 %collective-permute-start.4 = (bf16[2,512,128]{2,1,0:T(8,128)(2,1)}, bf16[2,512,128]{2,1,0:T(8,128)(2,1)}, u32[]{:S(2)}, u32[]{:S(2)}) collective-permute-start(bf16[2,512,128]{2,1,0:T(8,128)(2,1)} %pad_maximum_fusion), channel_id=1, source_target_pairs={{0,40},{8,48},{16,56},{24,64},{32,72},{40,80},{48,88},{56,96},{64,... | collective-permute-start | bytes 786440 | tf_op jit(solution)/shard_map/ppermute | solution.py:26
  74.0 3.4 %collective-permute-start.1 = (bf16[2,512,128]{2,1,0:T(8,128)(2,1)}, bf16[2,512,128]{2,1,0:T(8,128)(2,1)}, u32[]{:S(2)}, u32[]{:S(2)}) collective-permute-start(bf16[2,512,128]{2,1,0:T(8,128)(2,1)} %pad_maximum_fusion), channel_id=1, source_target_pairs={{0,16},{8,24},{16,32},{24,40},{32,48},{40,56},{48,64},{56,72},{64,... | collective-permute-start | bytes 786440 | tf_op jit(solution)/shard_map/ppermute | solution.py:26
  78.4 109.8 %collective-permute-done.1 = bf16[2,512,128]{2,1,0:T(8,128)(2,1)} collective-permute-done((bf16[2,512,128]{2,1,0:T(8,128)(2,1)}, bf16[2,512,128]{2,1,0:T(8,128)(2,1)}, u32[]{:S(2)}, u32[]{:S(2)}) %collective-permute-start.1) | collective-permute-done | bytes 262176 | tf_op jit(solution)/shard_map/ppermute | solution.py:26
  188.2 5.8 %collective-permute-start.2 = (bf16[2,512,128]{2,1,0:T(8,128)(2,1)}, bf16[2,512,128]{2,1,0:T(8,128)(2,1)S(1)}, u32[]{:S(2)}, u32[]{:S(2)}) collective-permute-start(bf16[2,512,128]{2,1,0:T(8,128)(2,1)} %pad_maximum_fusion), channel_id=1, source_target_pairs={{0,24},{8,32},{16,40},{24,48},{32,56},{40,64},{48,72},{56,80},{64,... | collective-permute-start | bytes 786440 | tf_op jit(solution)/shard_map/ppermute | solution.py:26
  194.0 1.8 fusion.2
  195.8 10.9 %collective-permute-done.2 = bf16[2,512,128]{2,1,0:T(8,128)(2,1)S(1)} collective-permute-done((bf16[2,512,128]{2,1,0:T(8,128)(2,1)}, bf16[2,512,128]{2,1,0:T(8,128)(2,1)S(1)}, u32[]{:S(2)}, u32[]{:S(2)}) %collective-permute-start.2) | collective-permute-done | bytes 262176 | tf_op jit(solution)/shard_map/ppermute | solution.py:26
  206.7 11.1 %collective-permute-start.3 = (bf16[2,512,128]{2,1,0:T(8,128)(2,1)}, bf16[2,512,128]{2,1,0:T(8,128)(2,1)S(1)}, u32[]{:S(2)}, u32[]{:S(2)}) collective-permute-start(bf16[2,512,128]{2,1,0:T(8,128)(2,1)} %pad_maximum_fusion), channel_id=1, source_target_pairs={{0,32},{8,40},{16,48},{24,56},{32,64},{40,72},{48,80},{56,88},{64,... | collective-permute-start | bytes 786440 | tf_op jit(solution)/shard_map/ppermute | solution.py:26
  218.7 7.8 %collective-permute-done.3 = bf16[2,512,128]{2,1,0:T(8,128)(2,1)S(1)} collective-permute-done((bf16[2,512,128]{2,1,0:T(8,128)(2,1)}, bf16[2,512,128]{2,1,0:T(8,128)(2,1)S(1)}, u32[]{:S(2)}, u32[]{:S(2)}) %collective-permute-start.3) | collective-permute-done | bytes 262176 | tf_op jit(solution)/shard_map/ppermute | solution.py:26
  226.4 9.1 %collective-permute-start = (bf16[2,512,128]{2,1,0:T(8,128)(2,1)}, bf16[2,512,128]{2,1,0:T(8,128)(2,1)S(1)}, u32[]{:S(2)}, u32[]{:S(2)}) collective-permute-start(bf16[2,512,128]{2,1,0:T(8,128)(2,1)} %pad_maximum_fusion), channel_id=1, source_target_pairs={{0,8},{8,16},{16,24},{24,32},{32,40},{40,48},{48,56},{56,64},{64,7... | collective-permute-start | bytes 786440 | tf_op jit(solution)/shard_map/ppermute | solution.py:26
  236.5 1.8 fusion.5
  238.3 1.8 fusion.6
  240.1 5.1 %collective-permute-done = bf16[2,512,128]{2,1,0:T(8,128)(2,1)S(1)} collective-permute-done((bf16[2,512,128]{2,1,0:T(8,128)(2,1)}, bf16[2,512,128]{2,1,0:T(8,128)(2,1)S(1)}, u32[]{:S(2)}, u32[]{:S(2)}) %collective-permute-start) | collective-permute-done | bytes 262176 | tf_op jit(solution)/shard_map/ppermute | solution.py:26
  246.2 1.8 fusion.7
  248.0 1.8 fusion.8
  259.6 2.1 fusion.93
  261.6 2.4 fusion.66
  264.0 2.4 fusion.69
  266.4 2.4 fusion.72
  268.9 1.5 fusion.75
  271.9 2.4 fusion.81
  274.3 3.2 fusion.141
  277.5 2.9 divide_convert_fusion
  281.8 50.9 %all_to_all.42 = bf16[64,8,512]{2,1,0:T(8,128)(2,1)S(1)} all-to-all(bf16[64,8,512]{2,1,0:T(8,128)(2,1)S(1)} %broadcast_select_fusion), channel_id=1, replica_groups=mesh['ctx'=64,'head'=8] {'ctx'}, dimensions={0} | all-to-all | bytes 1048576 | tf_op jit(solution)/shard_map/all_to_all | solution.py:124
  (73 shorter events, 33.0 us)
Async XLA Ops:
  0.0 0.9 copy-start
  1.6 24.3 %all-to-all-start.2 = ((bf16[64,8,128]{2,0,1:T(8,128)(2,1)}), bf16[64,8,128]{2,0,1:T(8,128)(2,1)S(1)}, u32[]{:S(2)}, u32[]{:S(2)}) async-start(bf16[64,8,128]{2,0,1:T(8,128)(2,1)} %copy_bitcast_fusion.1), calls=%async_computation.2 | async-start | bytes 262144 | tf_op jit(solution)/shard_map/all_to_all | solution.py:38
  25.9 8.2 %all-to-all-start = ((bf16[8,64,128]{2,1,0:T(8,128)(2,1)}), bf16[8,64,128]{2,1,0:T(8,128)(2,1)S(1)}, u32[]{:S(2)}, u32[]{:S(2)}) async-start(bf16[8,64,128]{2,1,0:T(8,128)(2,1)} %constant_dynamic-update-slice_fusion), calls=%async_computation | async-start | bytes 262144 | tf_op jit(solution)/shard_map/all_to_all | solution.py:15
  34.1 43.2 %all-to-all-start.1 = ((bf16[64,8,512]{2,0,1:T(8,128)(2,1)}), bf16[64,8,512]{2,0,1:T(8,128)(2,1)S(1)}, u32[]{:S(2)}, u32[]{:S(2)}) async-start(bf16[64,8,512]{2,0,1:T(8,128)(2,1)} %bitcast.471), calls=%async_computation.1 | async-start | bytes 1048576 | tf_op jit(solution)/shard_map/all_to_all | solution.py:36
  42.2 205.8 %collective-permute-start.7 = (bf16[2,512,128]{2,1,0:T(8,128)(2,1)}, bf16[2,512,128]{2,1,0:T(8,128)(2,1)}, u32[]{:S(2)}, u32[]{:S(2)}) collective-permute-start(bf16[2,512,128]{2,1,0:T(8,128)(2,1)} %pad_maximum_fusion), channel_id=1, source_target_pairs={{0,64},{8,72},{16,80},{24,88},{32,96},{40,104},{48,112},{56,120},{... | collective-permute-start | bytes 786440 | tf_op jit(solution)/shard_map/ppermute | solution.py:26
  54.3 191.9 %collective-permute-start.6 = (bf16[2,512,128]{2,1,0:T(8,128)(2,1)}, bf16[2,512,128]{2,1,0:T(8,128)(2,1)}, u32[]{:S(2)}, u32[]{:S(2)}) collective-permute-start(bf16[2,512,128]{2,1,0:T(8,128)(2,1)} %pad_maximum_fusion), channel_id=1, source_target_pairs={{0,56},{8,64},{16,72},{24,80},{32,88},{40,96},{48,104},{56,112},{6... | collective-permute-start | bytes 786440 | tf_op jit(solution)/shard_map/ppermute | solution.py:26
  60.7 177.6 %collective-permute-start.5 = (bf16[2,512,128]{2,1,0:T(8,128)(2,1)}, bf16[2,512,128]{2,1,0:T(8,128)(2,1)}, u32[]{:S(2)}, u32[]{:S(2)}) collective-permute-start(bf16[2,512,128]{2,1,0:T(8,128)(2,1)} %pad_maximum_fusion), channel_id=1, source_target_pairs={{0,48},{8,56},{16,64},{24,72},{32,80},{40,88},{48,96},{56,104},{64... | collective-permute-start | bytes 786440 | tf_op jit(solution)/shard_map/ppermute | solution.py:26
  65.3 171.1 %collective-permute-start.4 = (bf16[2,512,128]{2,1,0:T(8,128)(2,1)}, bf16[2,512,128]{2,1,0:T(8,128)(2,1)}, u32[]{:S(2)}, u32[]{:S(2)}) collective-permute-start(bf16[2,512,128]{2,1,0:T(8,128)(2,1)} %pad_maximum_fusion), channel_id=1, source_target_pairs={{0,40},{8,48},{16,56},{24,64},{32,72},{40,80},{48,88},{56,96},{64,... | collective-permute-start | bytes 786440 | tf_op jit(solution)/shard_map/ppermute | solution.py:26
  74.0 114.2 %collective-permute-start.1 = (bf16[2,512,128]{2,1,0:T(8,128)(2,1)}, bf16[2,512,128]{2,1,0:T(8,128)(2,1)}, u32[]{:S(2)}, u32[]{:S(2)}) collective-permute-start(bf16[2,512,128]{2,1,0:T(8,128)(2,1)} %pad_maximum_fusion), channel_id=1, source_target_pairs={{0,16},{8,24},{16,32},{24,40},{32,48},{40,56},{48,64},{56,72},{64,... | collective-permute-start | bytes 786440 | tf_op jit(solution)/shard_map/ppermute | solution.py:26
  188.2 18.5 %collective-permute-start.2 = (bf16[2,512,128]{2,1,0:T(8,128)(2,1)}, bf16[2,512,128]{2,1,0:T(8,128)(2,1)S(1)}, u32[]{:S(2)}, u32[]{:S(2)}) collective-permute-start(bf16[2,512,128]{2,1,0:T(8,128)(2,1)} %pad_maximum_fusion), channel_id=1, source_target_pairs={{0,24},{8,32},{16,40},{24,48},{32,56},{40,64},{48,72},{56,80},{64,... | collective-permute-start | bytes 786440 | tf_op jit(solution)/shard_map/ppermute | solution.py:26
  206.7 28.9 %copy-start.4 = (bf16[2,512,128]{2,1,0:T(8,128)(2,1)}, bf16[2,512,128]{2,1,0:T(8,128)(2,1)S(1)}, u32[]{:S(2)}) copy-start(bf16[2,512,128]{2,1,0:T(8,128)(2,1)S(1)} %collective-permute-done.2) | copy-start | bytes 786436
  206.7 19.8 %collective-permute-start.3 = (bf16[2,512,128]{2,1,0:T(8,128)(2,1)}, bf16[2,512,128]{2,1,0:T(8,128)(2,1)S(1)}, u32[]{:S(2)}, u32[]{:S(2)}) collective-permute-start(bf16[2,512,128]{2,1,0:T(8,128)(2,1)} %pad_maximum_fusion), channel_id=1, source_target_pairs={{0,32},{8,40},{16,48},{24,56},{32,64},{40,72},{48,80},{56,88},{64,... | collective-permute-start | bytes 786440 | tf_op jit(solution)/shard_map/ppermute | solution.py:26
  226.4 11.9 %copy-start.6 = (bf16[2,512,128]{2,1,0:T(8,128)(2,1)}, bf16[2,512,128]{2,1,0:T(8,128)(2,1)S(1)}, u32[]{:S(2)}) copy-start(bf16[2,512,128]{2,1,0:T(8,128)(2,1)S(1)} %collective-permute-done.3) | copy-start | bytes 786436
  226.4 18.8 %collective-permute-start = (bf16[2,512,128]{2,1,0:T(8,128)(2,1)}, bf16[2,512,128]{2,1,0:T(8,128)(2,1)S(1)}, u32[]{:S(2)}, u32[]{:S(2)}) collective-permute-start(bf16[2,512,128]{2,1,0:T(8,128)(2,1)} %pad_maximum_fusion), channel_id=1, source_target_pairs={{0,8},{8,16},{16,24},{24,32},{32,40},{40,48},{48,56},{56,64},{64,7... | collective-permute-start | bytes 786440 | tf_op jit(solution)/shard_map/ppermute | solution.py:26
  235.5 2.8 copy-start.1
  245.3 2.7 copy-start.2
  266.4 2.5 copy-start.7
  268.9 1.5 copy-start.5
  271.9 2.4 copy-start.3
